TPU v7x, 32 devices: a whole 2x2x4 slice. The times are simulated.
32 devices in a mesh: rep: 2 (over y), seq: 8 (over z, x), head: 2 (over core).
Axes of the slice: x: 2, y: 2, z: 4, core: 2. Of those that a mesh axis runs over, the one named last changes fastest.
Arguments:
- x_in: bfloat16 [1024, 1024], P(('rep', 'seq'), 'head'), parts along dimension 0, may hold values from -6 to 6
- b_in: bfloat16 [1024, 2048], P(('rep', 'seq'), 'head'), parts along dimension 0, may hold values from -6 to 6
- c_in: bfloat16 [1024, 2048], P(('rep', 'seq'), 'head'), parts along dimension 0, may hold values from -6 to 6
- z_in: bfloat16 [1024, 1024], P(('rep', 'seq'), 'head'), parts along dimension 0, may hold values from -6 to 6
- dt_raw: bfloat16 [1024, 16], P(('rep', 'seq'), 'head'), parts along dimension 0, may hold values from -3 to 6
- dt_bias: float32 [16], P('head'), may hold values from -4 to -3
- a_log: float32 [16], P('head')
- d_skip: float32 [16], P('head'), may hold values from 0.5 to 1.5
- conv_x: bfloat16 [4, 1024], P(None, 'head'), may hold values from -3 to 3
- conv_b: bfloat16 [4, 2048], P(None, 'head'), may hold values from -3 to 3
- conv_c: bfloat16 [4, 2048], P(None, 'head'), may hold values from -3 to 3
- norm_gain: float32 [1024], P('head'), may hold values from 0.5 to 1.5
Outputs:
- mixed: bfloat16 [1024, 1024], P(('rep', 'seq'), 'head'), parts along dimension 0
There are 2 independent parts, one for each index of `rep`. A program takes and returns all parts, laid end to end along the dimension named above; an argument that names none is the same for every part. Nothing has to cross between parts.
All inputs are finite; a program needn't handle non-finite values.
Results may differ from a plain program's by a relative error of at most 0.0051.
Values may be sent and summed in bfloat16 or wider, within the bound.
No kernel may reach another device: no remote copies, remote signals or barrier semaphores. Data moves between devices by JAX's collectives and lax.ppermute only.
A program may use at most 64 MiB of HBM per device.

v0:
```python
import jax
import jax.numpy as jnp
from jax import lax
from jax.sharding import PartitionSpec as P

HEAD_DIM = 64
STATE = 256
BLOCK = 256


def causal_conv(padded, kernel, length):
    summed = jnp.zeros((length,) + padded.shape[1:], jnp.float32)
    for offset in range(kernel.shape[0]):
        summed = summed + kernel[offset].astype(jnp.float32) * padded[
            offset : offset + length
        ].astype(jnp.float32)
    return jax.nn.silu(summed).astype(jnp.bfloat16)


def blockwise_scan(x_head, b_head, c_head, rates, decays):
    length = x_head.shape[0]
    blocks = length // BLOCK
    x_part = x_head.reshape(blocks, BLOCK, -1)
    b_part = b_head.reshape(blocks, BLOCK, -1)
    c_part = c_head.reshape(blocks, BLOCK, -1)
    rate_part = rates.reshape(blocks, BLOCK)
    log_decay = jnp.cumsum(decays.reshape(blocks, BLOCK), axis=1)
    causal = jnp.arange(BLOCK)[:, None] >= jnp.arange(BLOCK)[None, :]
    scores = jnp.einsum("cin,cjn->cij", c_part, b_part, preferred_element_type=jnp.float32)
    spread = jnp.where(causal, log_decay[:, :, None] - log_decay[:, None, :], 0.0)
    mixing = jnp.where(causal, scores * jnp.exp(spread) * rate_part[:, None, :], 0.0).astype(
        jnp.bfloat16
    )
    inner = jnp.einsum("cij,cjp->cip", mixing, x_part, preferred_element_type=jnp.float32)
    weighted_b = (
        b_part.astype(jnp.float32)
        * (jnp.exp(log_decay[:, -1:] - log_decay) * rate_part)[:, :, None]
    ).astype(jnp.bfloat16)
    block_states = jnp.einsum(
        "cjn,cjp->cnp", weighted_b, x_part, preferred_element_type=jnp.float32
    )
    totals = log_decay[:, -1]

    def carry_step(state, pair):
        total, fresh = pair
        return (jnp.exp(total) * state + fresh, state)

    final_state, entering = lax.scan(
        carry_step, jnp.zeros(block_states.shape[1:], jnp.float32), (totals, block_states)
    )
    entering_low = entering.astype(jnp.bfloat16)
    outer = jnp.exp(log_decay)[:, :, None] * jnp.einsum(
        "cin,cnp->cip", c_part, entering_low, preferred_element_type=jnp.float32
    )
    return (inner + outer).reshape(length, -1)


def body(x_in, b_in, c_in, z_in, dt_raw, dt_bias, a_log, d_skip, conv_x, conv_b, conv_c, norm_gain):
    local_rows = x_in.shape[0]
    seq_total = lax.axis_size("seq")
    seq_place = lax.axis_index("seq")
    heads_here = dt_raw.shape[1]
    per_device = heads_here // seq_total
    groups_here = b_in.shape[1] // STATE
    per_group = heads_here // groups_here
    kernel_taps = conv_x.shape[0]

    def widen(groupwise, last_dim):
        row_total = groupwise.shape[0]
        copies = jnp.broadcast_to(
            groupwise.reshape(row_total, groups_here, 1, last_dim),
            (row_total, groups_here, per_group, last_dim),
        )
        return copies.reshape(row_total, seq_total, per_device, last_dim)

    x_send, b_send, c_send = (x_in, b_in, c_in)
    outgoing = (
        x_send.reshape(local_rows, seq_total, per_device, HEAD_DIM),
        widen(b_send, STATE),
        widen(c_send, STATE),
        dt_raw.reshape(local_rows, seq_total, per_device),
    )
    arrived = (
        lax.all_to_all(outgoing[0], "seq", split_axis=1, concat_axis=0, tiled=True),
        lax.all_to_all(outgoing[1], "seq", split_axis=1, concat_axis=0, tiled=True),
        lax.all_to_all(outgoing[2], "seq", split_axis=1, concat_axis=0, tiled=True),
        lax.all_to_all(outgoing[3], "seq", split_axis=1, concat_axis=0, tiled=True),
    )
    length = local_rows * seq_total
    x_heads = arrived[0].reshape(length, per_device, HEAD_DIM)
    b_heads = arrived[1].reshape(length, per_device, STATE)
    c_heads = arrived[2].reshape(length, per_device, STATE)
    raw_rates = arrived[3].reshape(length, per_device)
    kernel_x = lax.dynamic_index_in_dim(
        conv_x.reshape(kernel_taps, seq_total, per_device, HEAD_DIM), seq_place, 1, keepdims=False
    )
    kernel_b = lax.dynamic_index_in_dim(widen(conv_b, STATE), seq_place, 1, keepdims=False)
    kernel_c = lax.dynamic_index_in_dim(widen(conv_c, STATE), seq_place, 1, keepdims=False)
    front = ((kernel_taps - 1, 0), (0, 0), (0, 0))
    x_heads = causal_conv(jnp.pad(x_heads, front), kernel_x, length)
    b_heads = causal_conv(jnp.pad(b_heads, front), kernel_b, length)
    c_heads = causal_conv(jnp.pad(c_heads, front), kernel_c, length)
    first_head = seq_place * per_device
    bias_here = lax.dynamic_slice_in_dim(dt_bias, first_head, per_device)
    alog_here = lax.dynamic_slice_in_dim(a_log, first_head, per_device)
    skip_here = lax.dynamic_slice_in_dim(d_skip, first_head, per_device)
    rates = jax.nn.softplus(raw_rates.astype(jnp.float32) + bias_here[None, :])
    decays = rates * (-jnp.exp(alog_here))[None, :]
    scanned = jax.vmap(blockwise_scan, in_axes=1, out_axes=1)(
        x_heads, b_heads, c_heads, rates, decays
    )
    heads_out = (scanned + skip_here[None, :, None] * x_heads.astype(jnp.float32)).astype(
        jnp.bfloat16
    )
    returned = lax.all_to_all(
        heads_out.reshape(length, 1, per_device, HEAD_DIM),
        "seq",
        split_axis=0,
        concat_axis=1,
        tiled=True,
    )
    merged = returned.reshape(local_rows, heads_here * HEAD_DIM).astype(jnp.float32)
    gated = merged * jax.nn.silu(z_in.astype(jnp.float32))
    grouped = gated.reshape(local_rows, groups_here, -1)
    mean_square = jnp.mean(grouped * grouped, axis=-1, keepdims=True)
    normed = (grouped * lax.rsqrt(mean_square + 1e-05)).reshape(local_rows, -1)
    return (normed * norm_gain[None, :]).astype(jnp.bfloat16)


def solution(mesh):
    placed = (
        P(("rep", "seq"), "head"),
        P(("rep", "seq"), "head"),
        P(("rep", "seq"), "head"),
        P(("rep", "seq"), "head"),
        P(("rep", "seq"), "head"),
        P("head"),
        P("head"),
        P("head"),
        P(None, "head"),
        P(None, "head"),
        P(None, "head"),
        P("head"),
    )
    return jax.shard_map(
        body, mesh=mesh, in_specs=placed, out_specs=P(("rep", "seq"), "head"), check_vma=False
    )
```

profile of v0, /device:TPU:0, one launch (start us, length us, event | category | flops | bytes accessed | tf_op | source)
XLA Modules:
  0.0 69.4 jit_solution(514059991303077825)
XLA Ops:
  0.0 1.3 %copy.99 = bf16[64,8,1]{0,2,1:T(2,128)(2,1)} copy(bf16[64,8,1]{0,1,2:T(8,128)(2,1)} %bitcast.160) | data formatting | bytes 2048 | tf_op jit(solution)/shard_map/reshape | solution.py:81
  1.3 7.3 %all-to-all-start.2 = ((bf16[64,8,1]{0,2,1:T(2,128)(2,1)}), bf16[64,8,1]{0,2,1:T(2,128)(2,1)S(1)}, u32[]{:S(2)}, u32[]{:S(2)}) async-start(bf16[64,8,1]{0,2,1:T(2,128)(2,1)} %copy.99), calls=%async_computation.2 | async-start | bytes 8192 | tf_op jit(solution)/shard_map/all_to_all | solution.py:87
  8.6 0.6 copy-done.4
  9.4 0.7 copy-done.6
  10.2 0.6 copy-done.8
  10.8 0.6 dynamic_slice.30
  11.5 0.6 dynamic_slice.31
  12.8 0.8 %copy-done.3 = bf16[64,512]{1,0:T(8,128)(2,1)S(1)} copy-done((bf16[64,512]{1,0:T(8,128)(2,1)S(1)}, bf16[64,512]{1,0:T(8,128)(2,1)}, u32[]{:S(2)}) %copy-start.3) | copy-done | bytes 65560
  13.8 0.8 %reshape.665 = bf16[8,2,2048]{2,1,0:T(2,128)(2,1)} reshape(bf16[8,1,64,64]{3,2,1,0:T(8,128)(2,1)S(1)} %bitcast.145) | data formatting | bytes 131072
  14.7 0.6 copy-done.10
  15.3 0.6 dynamic_slice.33
  15.9 6.0 %all-to-all-start.3 = ((bf16[8,2,2048]{2,1,0:T(2,128)(2,1)}), bf16[8,2,2048]{2,1,0:T(2,128)(2,1)S(1)}, u32[]{:S(2)}, u32[]{:S(2)}) async-start(bf16[8,2,2048]{2,1,0:T(2,128)(2,1)} %reshape.665), calls=%async_computation.3 | async-start | bytes 131072 | tf_op jit(solution)/shard_map/all_to_all | solution.py:84
  21.9 0.6 convert_add_fusion
  22.6 0.6 reduce-window.6
  24.0 4.8 %all-to-all-done.3 = bf16[8,2,2048]{2,1,0:T(2,128)(2,1)S(1)} async-done(((bf16[8,2,2048]{2,1,0:T(2,128)(2,1)}), bf16[8,2,2048]{2,1,0:T(2,128)(2,1)S(1)}, u32[]{:S(2)}, u32[]{:S(2)}) %all-to-all-start.3) | async-done | bytes 65568 | tf_op jit(solution)/shard_map/all_to_all | solution.py:84
  28.8 0.7 %broadcast_in_dim.82 = bf16[64,4,2,256]{3,0,2,1:T(8,128)(2,1)} broadcast(bf16[64,4,256]{2,0,1:T(8,128)(2,1)S(1)} %bitcast.144), dimensions={0,1,3} | broadcast | bytes 393216 | tf_op jit(solution)/shard_map/broadcast_in_dim | solution.py:70
  29.5 3.4 %all-to-all-start.1 = ((bf16[64,8,1,256]{3,0,2,1:T(8,128)(2,1)}), bf16[64,8,1,256]{3,0,2,1:T(8,128)(2,1)S(1)}, u32[]{:S(2)}, u32[]{:S(2)}) async-start(bf16[64,8,1,256]{3,0,2,1:T(8,128)(2,1)} %bitcast.12), calls=%async_computation.1 | async-start | bytes 524288 | tf_op jit(solution)/shard_map/all_to_all | solution.py:85
  33.7 7.5 %all-to-all-done.1 = bf16[64,8,1,256]{3,0,2,1:T(8,128)(2,1)S(1)} async-done(((bf16[64,8,1,256]{3,0,2,1:T(8,128)(2,1)}), bf16[64,8,1,256]{3,0,2,1:T(8,128)(2,1)S(1)}, u32[]{:S(2)}, u32[]{:S(2)}) %all-to-all-start.1) | async-done | bytes 262176 | tf_op jit(solution)/shard_map/all_to_all | solution.py:85
  41.1 0.7 %broadcast_in_dim.41 = bf16[64,4,2,256]{3,0,2,1:T(8,128)(2,1)} broadcast(bf16[64,4,256]{2,0,1:T(8,128)(2,1)S(1)} %bitcast.143), dimensions={0,1,3} | broadcast | bytes 393216 | tf_op jit(solution)/shard_map/broadcast_in_dim | solution.py:70
  41.8 3.4 %all-to-all-start = ((bf16[64,8,1,256]{3,0,2,1:T(8,128)(2,1)}), bf16[64,8,1,256]{3,0,2,1:T(8,128)(2,1)S(1)}, u32[]{:S(2)}, u32[]{:S(2)}) async-start(bf16[64,8,1,256]{3,0,2,1:T(8,128)(2,1)} %bitcast.1), calls=%async_computation | async-start | bytes 524288 | tf_op jit(solution)/shard_map/all_to_all | solution.py:86
  45.9 2.9 %while.13 = (s32[]{:T(128)}, f32[1,256,64]{2,1,0:T(8,128)S(1)}, bf16[2,1,256,64]{3,2,1,0:T(8,128)(2,1)S(1)}, f32[2,1]{0,1:T(1,128)S(1)}, f32[2,1,256,64]{2,3,0,1:T(8,128)S(1)}, /*index=5*/s32[]{:T(128)}, s32[]{:T(128)}) while((s32[]{:T(128)}, f32[1,256,64]{2,1,0:T(8,128)S(1)}, bf16[2,1,256,64]{3,2,1,0:T(8,128)(2,1)S(1)}, ...), condition=%wide.region_3.4_spmd.clone, body=%wide.region_2.3_spmd.clone.sunk | while | flops 65539 | bytes 655472 | solution.py:48
  46.1 0.6 fusion.52
  46.6 0.7 bitcast_add_fusion.4
  47.5 0.6 fusion.52
  48.1 0.7 bitcast_add_fusion.4
  48.8 4.6 %all-to-all-done = bf16[64,8,1,256]{3,0,2,1:T(8,128)(2,1)S(1)} async-done(((bf16[64,8,1,256]{3,0,2,1:T(8,128)(2,1)}), bf16[64,8,1,256]{3,0,2,1:T(8,128)(2,1)S(1)}, u32[]{:S(2)}, u32[]{:S(2)}) %all-to-all-start) | async-done | bytes 262176 | tf_op jit(solution)/shard_map/all_to_all | solution.py:86
  54.6 0.8 %fusion.22 = bf16[512,1,1,64]{0,3,2,1:T(8,128)(2,1)S(1)} fusion(f32[512,1,64]{0,2,1:T(8,128)S(1)} %reshape.647, f32[]{:T(128)} %bitcast.43, bf16[512,1,64]{0,2,1:T(8,128)(2,1)S(1)} %reshape.642, f32[64]{0:T(128)S(1)} %get-tuple-element.105, f32[64]{0:T(128)S(1)} %get-tuple-element.103, f32[64]{0:T(128)S(1)} %get-tuple-element.104, f32[64]{0:T(128)S(1)} %get-tuple-element.102), kind=kLoop, calls=%fused_computation.45 | loop fusion | flops 655360 | bytes 263172 | tf_op jit(solution)/shard_map/reshape | solution.py:116
  55.9 0.7 reduce.2
  56.9 9.6 %all_to_all.63 = bf16[8,2,2048]{2,1,0:T(2,128)(2,1)S(1)} all-to-all(bf16[8,2,2048]{2,1,0:T(2,128)(2,1)S(1)} %reshape.667), channel_id=1, replica_groups=mesh['rep'=2,'seq'=8,'head'=2] {'seq'}, dimensions={0} | all-to-all | bytes 131072 | tf_op jit(solution)/shard_map/all_to_all | solution.py:115
  67.1 0.7 %copy-done = bf16[64,512]{1,0:T(8,128)(2,1)S(1)} copy-done((bf16[64,512]{1,0:T(8,128)(2,1)S(1)}, bf16[64,512]{1,0:T(8,128)(2,1)}, u32[]{:S(2)}) %copy-start) | copy-done | bytes 65560
  68.2 0.5 copy-done.7
  68.8 0.7 fusion.19
  (76 shorter events, 5.9 us)
Async XLA Ops:
  1.3 14.6 %all-to-all-start.2 = ((bf16[64,8,1]{0,2,1:T(2,128)(2,1)}), bf16[64,8,1]{0,2,1:T(2,128)(2,1)S(1)}, u32[]{:S(2)}, u32[]{:S(2)}) async-start(bf16[64,8,1]{0,2,1:T(2,128)(2,1)} %copy.99), calls=%async_computation.2 | async-start | bytes 8192 | tf_op jit(solution)/shard_map/all_to_all | solution.py:87
  8.6 0.7 %copy-start.4 = (bf16[4,1024]{1,0:T(4,128)(2,1)S(1)}, bf16[4,1024]{1,0:T(4,128)(2,1)}, u32[]{:S(2)}) copy-start(bf16[4,1024]{1,0:T(4,128)(2,1)} %param.24) | copy-start | bytes 24580
  8.6 0.7 %copy-start.5 = (bf16[4,1024]{1,0:T(4,128)(2,1)S(1)}, bf16[4,1024]{1,0:T(4,128)(2,1)}, u32[]{:S(2)}) copy-start(bf16[4,1024]{1,0:T(4,128)(2,1)} %param.23) | copy-start | bytes 24580
  8.6 4.2 %copy-start.1 = (bf16[64,1024]{1,0:T(8,128)(2,1)S(1)}, bf16[64,1024]{1,0:T(8,128)(2,1)}, u32[]{:S(2)}) copy-start(bf16[64,1024]{1,0:T(8,128)(2,1)} %param.15) | copy-start | bytes 393220
  9.3 0.7 copy-start.6
  10.2 0.7 copy-start.8
  10.8 0.7 copy-start.9
  12.8 0.8 %copy-start.3 = (bf16[64,512]{1,0:T(8,128)(2,1)S(1)}, bf16[64,512]{1,0:T(8,128)(2,1)}, u32[]{:S(2)}) copy-start(bf16[64,512]{1,0:T(8,128)(2,1)} %param.14) | copy-start | bytes 196612
  13.8 0.9 %copy-start.2 = (bf16[64,1024]{1,0:T(8,128)(2,1)S(1)}, bf16[64,1024]{1,0:T(8,128)(2,1)}, u32[]{:S(2)}) copy-start(bf16[64,1024]{1,0:T(8,128)(2,1)} %param.16) | copy-start | bytes 393220
  14.7 0.7 copy-start.10
  15.9 12.9 %all-to-all-start.3 = ((bf16[8,2,2048]{2,1,0:T(2,128)(2,1)}), bf16[8,2,2048]{2,1,0:T(2,128)(2,1)S(1)}, u32[]{:S(2)}, u32[]{:S(2)}) async-start(bf16[8,2,2048]{2,1,0:T(2,128)(2,1)} %reshape.665), calls=%async_computation.3 | async-start | bytes 131072 | tf_op jit(solution)/shard_map/all_to_all | solution.py:84
  29.5 11.6 %all-to-all-start.1 = ((bf16[64,8,1,256]{3,0,2,1:T(8,128)(2,1)}), bf16[64,8,1,256]{3,0,2,1:T(8,128)(2,1)S(1)}, u32[]{:S(2)}, u32[]{:S(2)}) async-start(bf16[64,8,1,256]{3,0,2,1:T(8,128)(2,1)} %bitcast.12), calls=%async_computation.1 | async-start | bytes 524288 | tf_op jit(solution)/shard_map/all_to_all | solution.py:85
  41.8 11.6 %all-to-all-start = ((bf16[64,8,1,256]{3,0,2,1:T(8,128)(2,1)}), bf16[64,8,1,256]{3,0,2,1:T(8,128)(2,1)S(1)}, u32[]{:S(2)}, u32[]{:S(2)}) async-start(bf16[64,8,1,256]{3,0,2,1:T(8,128)(2,1)} %bitcast.1), calls=%async_computation | async-start | bytes 524288 | tf_op jit(solution)/shard_map/all_to_all | solution.py:86
  67.0 0.8 %copy-start = (bf16[64,512]{1,0:T(8,128)(2,1)S(1)}, bf16[64,512]{1,0:T(8,128)(2,1)}, u32[]{:S(2)}) copy-start(bf16[64,512]{1,0:T(8,128)(2,1)} %param.17) | copy-start | bytes 196612
  68.1 0.7 copy-start.7
where the time goes:
time: 70.2 us; the launch traced here: 69.4 us
  starting transfers between devices  20.1 us (29%)
  waiting for transfers between devices  16.9 us (24%)
  local copies, waits for them, and re-layouts  14.7 us (21%)
  blocking collectives  9.55 us (14%)
  other arithmetic  6.17 us (9%)
  between operations  1.08 us (2%)
  matrix products  0.91 us (1%)
    all_to_all x1, blocking collectives, body(): lax.all_to_all(heads_out.reshape(length, 1, per_device, HEAD_DIM), 'seq',...  9.55 us
    all_to_all x1, waiting for transfers between devices, body(): lax.all_to_all(outgoing[1], 'seq', split_axis=1, concat_axis=0, tiled=True)  7.46 us
    all_to_all x1, starting transfers between devices, body(): lax.all_to_all(outgoing[3], 'seq', split_axis=1, concat_axis=0, tiled=True)  7.28 us
    unnamed x28, local copies, waits for them, and re-layouts  6.26 us
    all_to_all x1, starting transfers between devices, body(): lax.all_to_all(outgoing[0], 'seq', split_axis=1, concat_axis=0, tiled=True)  6 us
    all_to_all x1, waiting for transfers between devices, body(): lax.all_to_all(outgoing[0], 'seq', split_axis=1, concat_axis=0, tiled=True)  4.77 us
    all_to_all x1, waiting for transfers between devices, body(): lax.all_to_all(outgoing[2], 'seq', split_axis=1, concat_axis=0, tiled=True)  4.64 us
    all_to_all x1, starting transfers between devices, body(): lax.all_to_all(outgoing[1], 'seq', split_axis=1, concat_axis=0, tiled=True)  3.41 us
  transfers between devices with their start and end apart: 4, of which 3 were waited for; matrix products, arithmetic and copies ran while one was open for 13% of the time, Pallas kernels for 0%

commit v1 on v0

--- a/solution.py
+++ b/solution.py
@@ -84,7 +84,12 @@
         lax.all_to_all(outgoing[0], "seq", split_axis=1, concat_axis=0, tiled=True),
         lax.all_to_all(outgoing[1], "seq", split_axis=1, concat_axis=0, tiled=True),
         lax.all_to_all(outgoing[2], "seq", split_axis=1, concat_axis=0, tiled=True),
-        lax.all_to_all(outgoing[3], "seq", split_axis=1, concat_axis=0, tiled=True),
+        jnp.concatenate(
+            lax.all_to_all(
+                jnp.stack(jnp.split(outgoing[3], lax.axis_size("seq"), axis=1)), "seq", 0, 0
+            ),
+            axis=0,
+        ),
     )
     length = local_rows * seq_total
     x_heads = arrived[0].reshape(length, per_device, HEAD_DIM)

time: 70.2 us -> 74.2 us (1.057)
  local copies, waits for them, and re-layouts: 14.7 us -> 19.1 us
  waiting for transfers between devices: 16.9 us -> 15.7 us
  other arithmetic: 6.17 us -> 6.93 us
    unnamed x28 -> x37, local copies, waits for them, and re-layouts: 6.26 us -> 10.8 us
    reshape x1 -> x0, local copies, waits for them, and re-layouts: 1.28 us -> none  [body(): dt_raw.reshape(local_rows, seq_total, per_device)]
    all_to_all x1, waiting for transfers between devices: 4.77 us -> 3.58 us  [body(): lax.all_to_all(outgoing[0], 'seq', split_axis=1, concat_axis=0, tiled=True)]
  transfers between devices with their start and end apart: 4 -> 4, of which waited for: 3 -> 3; matrix products, arithmetic and copies ran while one was open for 13% -> 14% of each run, Pallas kernels for 0% -> 0%
where the time goes in v1:
time: 74.2 us; the launch traced here: 73.4 us
  starting transfers between devices  20.1 us (27%)
  local copies, waits for them, and re-layouts  19.1 us (26%)
  waiting for transfers between devices  15.7 us (21%)
  blocking collectives  9.55 us (13%)
  other arithmetic  6.93 us (9%)
  between operations  1.08 us (1%)
  matrix products  0.91 us (1%)
    unnamed x37, local copies, waits for them, and re-layouts  10.8 us
    all_to_all x1, blocking collectives, body(): lax.all_to_all(heads_out.reshape(length, 1, per_device, HEAD_DIM), 'seq',...  9.55 us
    all_to_all x1, waiting for transfers between devices, body(): lax.all_to_all(outgoing[1], 'seq', split_axis=1, concat_axis=0, tiled=True)  7.46 us
    all_to_all x1, starting transfers between devices, body(): lax.all_to_all(jnp.stack(jnp.split(outgoing[3], lax.axis_size('seq'), axi...  7.28 us
    all_to_all x1, starting transfers between devices, body(): lax.all_to_all(outgoing[0], 'seq', split_axis=1, concat_axis=0, tiled=True)  6 us
    all_to_all x1, waiting for transfers between devices, body(): lax.all_to_all(outgoing[2], 'seq', split_axis=1, concat_axis=0, tiled=True)  4.64 us
    all_to_all x1, waiting for transfers between devices, body(): lax.all_to_all(outgoing[0], 'seq', split_axis=1, concat_axis=0, tiled=True)  3.58 us
    all_to_all x1, starting transfers between devices, body(): lax.all_to_all(outgoing[1], 'seq', split_axis=1, concat_axis=0, tiled=True)  3.41 us
  transfers between devices with their start and end apart: 4, of which 3 were waited for; matrix products, arithmetic and copies ran while one was open for 14% of the time, Pallas kernels for 0%

profile of v1, /device:TPU:0, one launch (start us, length us, event | category | flops | bytes accessed | tf_op | source)
XLA Modules:
  0.0 73.4 jit_solution(9491784711515979295)
XLA Ops:
  0.0 1.3 %constant_dynamic-update-slice_fusion.7 = bf16[8,64,1,1]{1,3,2,0:T(2,128)(2,1)} fusion(bf16[64,8,1]{0,1,2:T(8,128)(2,1)} %bitcast.166), kind=kLoop, calls=%fused_computation.56 | loop fusion | bytes 640
  4.0 0.6 constant_dynamic-update-slice_fusion.1
  5.0 7.3 %all-to-all-start.2 = ((bf16[8,64,1,1]{1,3,2,0:T(2,128)(2,1)}), bf16[8,64,1,1]{1,3,2,0:T(2,128)(2,1)S(1)}, u32[]{:S(2)}, u32[]{:S(2)}) async-start(bf16[8,64,1,1]{1,3,2,0:T(2,128)(2,1)} %constant_dynamic-update-slice_fusion), calls=%async_computation.2 | async-start | bytes 8192 | tf_op jit(solution)/shard_map/all_to_all | solution.py:88
  12.4 0.6 copy-done.4
  13.1 0.7 copy-done.6
  14.0 0.6 copy-done.9
  14.6 0.6 dynamic_slice.30
  15.3 0.6 dynamic_slice.31
  16.6 0.8 %copy-done.3 = bf16[64,512]{1,0:T(8,128)(2,1)S(1)} copy-done((bf16[64,512]{1,0:T(8,128)(2,1)S(1)}, bf16[64,512]{1,0:T(8,128)(2,1)}, u32[]{:S(2)}) %copy-start.3) | copy-done | bytes 65560
  17.5 0.8 %reshape.669 = bf16[8,2,2048]{2,1,0:T(2,128)(2,1)} reshape(bf16[8,1,64,64]{3,2,1,0:T(8,128)(2,1)S(1)} %bitcast.152) | data formatting | bytes 131072
  18.4 0.6 copy-done.11
  19.1 0.7 dynamic_slice.33
  19.7 6.0 %all-to-all-start.3 = ((bf16[8,2,2048]{2,1,0:T(2,128)(2,1)}), bf16[8,2,2048]{2,1,0:T(2,128)(2,1)S(1)}, u32[]{:S(2)}, u32[]{:S(2)}) async-start(bf16[8,2,2048]{2,1,0:T(2,128)(2,1)} %reshape.669), calls=%async_computation.3 | async-start | bytes 131072 | tf_op jit(solution)/shard_map/all_to_all | solution.py:84
  26.3 1.3 %fusion.47 = (f32[8,64]{1,0:T(8,128)S(1)}, f32[8,64,1,1]{1,3,2,0:T(1,128)S(1)}) fusion(f32[]{:T(128)} %broadcast.202, f32[]{:T(128)} %bitcast.31, bf16[8,64,1,1]{1,3,2,0:T(2,128)(2,1)S(1)} %all-to-all-done.2), kind=kLoop, calls=%fused_computation.99 | loop fusion | flops 1024 | bytes 5128 | tf_op jit(solution)/shard_map/add | solution.py:112
  27.7 0.6 reduce-window.6
  29.1 3.6 %all-to-all-done.3 = bf16[8,2,2048]{2,1,0:T(2,128)(2,1)S(1)} async-done(((bf16[8,2,2048]{2,1,0:T(2,128)(2,1)}), bf16[8,2,2048]{2,1,0:T(2,128)(2,1)S(1)}, u32[]{:S(2)}, u32[]{:S(2)}) %all-to-all-start.3) | async-done | bytes 65568 | tf_op jit(solution)/shard_map/all_to_all | solution.py:84
  32.7 0.7 broadcast_in_dim.82
  33.4 3.4 %all-to-all-start.1 = ((bf16[64,8,1,256]{3,0,2,1:T(8,128)(2,1)}), bf16[64,8,1,256]{3,0,2,1:T(8,128)(2,1)S(1)}, u32[]{:S(2)}, u32[]{:S(2)}) async-start(bf16[64,8,1,256]{3,0,2,1:T(8,128)(2,1)} %bitcast.12), calls=%async_computation.1 | async-start | bytes 524288 | tf_op jit(solution)/shard_map/all_to_all | solution.py:85
  37.5 7.5 %all-to-all-done.1 = bf16[64,8,1,256]{3,0,2,1:T(8,128)(2,1)S(1)} async-done(((bf16[64,8,1,256]{3,0,2,1:T(8,128)(2,1)}), bf16[64,8,1,256]{3,0,2,1:T(8,128)(2,1)S(1)}, u32[]{:S(2)}, u32[]{:S(2)}) %all-to-all-start.1) | async-done | bytes 262176 | tf_op jit(solution)/shard_map/all_to_all | solution.py:85
  44.9 0.7 broadcast_in_dim.41
  45.7 3.4 %all-to-all-start = ((bf16[64,8,1,256]{3,0,2,1:T(8,128)(2,1)}), bf16[64,8,1,256]{3,0,2,1:T(8,128)(2,1)S(1)}, u32[]{:S(2)}, u32[]{:S(2)}) async-start(bf16[64,8,1,256]{3,0,2,1:T(8,128)(2,1)} %bitcast.1), calls=%async_computation | async-start | bytes 524288 | tf_op jit(solution)/shard_map/all_to_all | solution.py:86
  49.7 2.9 %while.13 = (s32[]{:T(128)}, f32[1,256,64]{2,1,0:T(8,128)S(1)}, bf16[2,1,256,64]{3,2,1,0:T(8,128)(2,1)S(1)}, f32[2,1]{0,1:T(1,128)S(1)}, f32[2,1,256,64]{2,3,0,1:T(8,128)S(1)}, /*index=5*/s32[]{:T(128)}, s32[]{:T(128)}) while((s32[]{:T(128)}, f32[1,256,64]{2,1,0:T(8,128)S(1)}, bf16[2,1,256,64]{3,2,1,0:T(8,128)(2,1)S(1)}, ...), condition=%wide.region_3.4_spmd.clone, body=%wide.region_2.3_spmd.clone.sunk | while | flops 65539 | bytes 655472 | solution.py:48
  49.9 0.6 fusion.53
  50.5 0.7 bitcast_add_fusion.4
  51.3 0.6 fusion.53
  51.9 0.7 bitcast_add_fusion.4
  52.6 4.6 %all-to-all-done = bf16[64,8,1,256]{3,0,2,1:T(8,128)(2,1)S(1)} async-done(((bf16[64,8,1,256]{3,0,2,1:T(8,128)(2,1)}), bf16[64,8,1,256]{3,0,2,1:T(8,128)(2,1)S(1)}, u32[]{:S(2)}, u32[]{:S(2)}) %all-to-all-start) | async-done | bytes 262176 | tf_op jit(solution)/shard_map/all_to_all | solution.py:86
  58.4 0.9 %fusion.22 = bf16[512,1,1,64]{0,3,2,1:T(8,128)(2,1)S(1)} fusion(f32[512,1,64]{0,2,1:T(8,128)S(1)} %reshape.639, f32[]{:T(128)} %bitcast.48, bf16[512,1,64]{0,2,1:T(8,128)(2,1)S(1)} %reshape.634, f32[64]{0:T(128)S(1)} %get-tuple-element.102, f32[64]{0:T(128)S(1)} %get-tuple-element.100, f32[64]{0:T(128)S(1)} %get-tuple-element.101, f32[64]{0:T(128)S(1)} %get-tuple-element.99), kind=kLoop, calls=%fused_computation.45 | loop fusion | flops 655360 | bytes 263172 | tf_op jit(solution)/shard_map/reshape | solution.py:121
  59.8 0.7 reduce.9
  60.8 9.6 %all_to_all.59 = bf16[8,2,2048]{2,1,0:T(2,128)(2,1)S(1)} all-to-all(bf16[8,2,2048]{2,1,0:T(2,128)(2,1)S(1)} %reshape.671), channel_id=1, replica_groups=mesh['rep'=2,'seq'=8,'head'=2] {'seq'}, dimensions={0} | all-to-all | bytes 131072 | tf_op jit(solution)/shard_map/all_to_all | solution.py:120
  71.0 0.7 copy-done
  72.7 0.7 fusion.19
  (86 shorter events, 10.1 us)
Async XLA Ops:
  0.0 1.3 %copy-start.8 = (bf16[64,8]{0,1:T(8,128)(2,1)S(1)}, bf16[64,8]{0,1:T(8,128)(2,1)}, u32[]{:S(2)}) copy-start(bf16[64,8]{0,1:T(8,128)(2,1)} %param.18) | copy-start | bytes 3076
  5.0 14.7 %all-to-all-start.2 = ((bf16[8,64,1,1]{1,3,2,0:T(2,128)(2,1)}), bf16[8,64,1,1]{1,3,2,0:T(2,128)(2,1)S(1)}, u32[]{:S(2)}, u32[]{:S(2)}) async-start(bf16[8,64,1,1]{1,3,2,0:T(2,128)(2,1)} %constant_dynamic-update-slice_fusion), calls=%async_computation.2 | async-start | bytes 8192 | tf_op jit(solution)/shard_map/all_to_all | solution.py:88
  12.3 0.7 copy-start.4
  12.3 0.7 %copy-start.5 = (bf16[4,1024]{1,0:T(4,128)(2,1)S(1)}, bf16[4,1024]{1,0:T(4,128)(2,1)}, u32[]{:S(2)}) copy-start(bf16[4,1024]{1,0:T(4,128)(2,1)} %param.23) | copy-start | bytes 24580
  12.4 4.2 %copy-start.1 = (bf16[64,1024]{1,0:T(8,128)(2,1)S(1)}, bf16[64,1024]{1,0:T(8,128)(2,1)}, u32[]{:S(2)}) copy-start(bf16[64,1024]{1,0:T(8,128)(2,1)} %param.15) | copy-start | bytes 393220
  13.1 0.7 copy-start.6
  13.9 0.7 copy-start.9
  14.6 0.7 copy-start.10
  16.5 0.8 %copy-start.3 = (bf16[64,512]{1,0:T(8,128)(2,1)S(1)}, bf16[64,512]{1,0:T(8,128)(2,1)}, u32[]{:S(2)}) copy-start(bf16[64,512]{1,0:T(8,128)(2,1)} %param.14) | copy-start | bytes 196612
  17.5 0.9 %copy-start.2 = (bf16[64,1024]{1,0:T(8,128)(2,1)S(1)}, bf16[64,1024]{1,0:T(8,128)(2,1)}, u32[]{:S(2)}) copy-start(bf16[64,1024]{1,0:T(8,128)(2,1)} %param.16) | copy-start | bytes 393220
  18.4 0.7 copy-start.11
  19.7 12.9 %all-to-all-start.3 = ((bf16[8,2,2048]{2,1,0:T(2,128)(2,1)}), bf16[8,2,2048]{2,1,0:T(2,128)(2,1)S(1)}, u32[]{:S(2)}, u32[]{:S(2)}) async-start(bf16[8,2,2048]{2,1,0:T(2,128)(2,1)} %reshape.669), calls=%async_computation.3 | async-start | bytes 131072 | tf_op jit(solution)/shard_map/all_to_all | solution.py:84
  33.4 11.6 %all-to-all-start.1 = ((bf16[64,8,1,256]{3,0,2,1:T(8,128)(2,1)}), bf16[64,8,1,256]{3,0,2,1:T(8,128)(2,1)S(1)}, u32[]{:S(2)}, u32[]{:S(2)}) async-start(bf16[64,8,1,256]{3,0,2,1:T(8,128)(2,1)} %bitcast.12), calls=%async_computation.1 | async-start | bytes 524288 | tf_op jit(solution)/shard_map/all_to_all | solution.py:85
  45.7 11.6 %all-to-all-start = ((bf16[64,8,1,256]{3,0,2,1:T(8,128)(2,1)}), bf16[64,8,1,256]{3,0,2,1:T(8,128)(2,1)S(1)}, u32[]{:S(2)}, u32[]{:S(2)}) async-start(bf16[64,8,1,256]{3,0,2,1:T(8,128)(2,1)} %bitcast.1), calls=%async_computation | async-start | bytes 524288 | tf_op jit(solution)/shard_map/all_to_all | solution.py:86
  70.9 0.8 %copy-start = (bf16[64,512]{1,0:T(8,128)(2,1)S(1)}, bf16[64,512]{1,0:T(8,128)(2,1)}, u32[]{:S(2)}) copy-start(bf16[64,512]{1,0:T(8,128)(2,1)} %param.17) | copy-start | bytes 196612
  72.0 0.7 copy-start.7
